TPU v7x, 32 devices: a whole 2x2x4 slice. The times are simulated.
32 devices in a mesh: inp: 8 (over z, core), tm: 4 (over y, x).
Axes of the slice: x: 2, y: 2, z: 4, core: 2. Of those that a mesh axis runs over, the one named last changes fastest.
Arguments:
- samples: bfloat16 [256, 786432], P('inp', 'tm'), may hold values from -6 to 6
- tap_weights: float32 [4, 512], replicated, may hold values from -3 to 3
Outputs:
- visibilities: float32 [256, 2, 256, 256], P('tm', None, 'inp')
All inputs are finite; a program needn't handle non-finite values.
Results may differ from a plain program's by a relative error of at most 0.00081.
Values may be sent and summed in bfloat16 or wider, within the bound.
A program may use at most 128 MiB of HBM per device.

v0:
```python
import math
import jax
import jax.numpy as jnp
from jax import lax
from jax.sharding import PartitionSpec as P


def passed_along(block, axis, distance):
    devices = range(lax.axis_size(axis))
    route = [(i - distance, i) for i in devices if i - distance in devices]
    return lax.ppermute(block, axis, route)


def filter_taps(extended, weights, count):
    total = weights[0][None, None, :] * extended[:, 0:count, :].astype(jnp.float32)
    for tap in range(1, weights.shape[0]):
        total = total + weights[tap][None, None, :] * extended[:, tap : tap + count, :].astype(
            jnp.float32
        )
    return total


def per_device(samples, tap_weights):
    in_dev = samples.shape[0]
    frame = tap_weights.shape[1]
    taps = tap_weights.shape[0]
    rim = taps - 1
    spectra_dev = samples.shape[1] // frame
    frames = samples.reshape(in_dev, spectra_dev, frame)
    before = passed_along(frames[:, spectra_dev - rim :, :], "tm", 1)
    filtered = filter_taps(jnp.concatenate([before, frames], axis=1), tap_weights, spectra_dev)
    n_inp = lax.axis_size("inp")
    n_time = lax.axis_size("tm")
    ch_dev = frame // 2 // n_inp
    column = jnp.arange(frame, dtype=jnp.int32)
    remain = column % (2 * ch_dev)
    channel = column // (2 * ch_dev) * ch_dev + remain % ch_dev
    is_real = remain // ch_dev == 0
    index_n = jnp.arange(frame, dtype=jnp.int32)
    phase = index_n[:, None] * channel[None, :] % frame
    angle = phase.astype(jnp.float32) * (2.0 * math.pi / frame)
    table = jnp.where(is_real[None, :], jnp.cos(angle), -jnp.sin(angle)) * frame ** (-0.5)
    spectra = jnp.einsum(
        "isn,nj->ijs",
        filtered,
        table,
        precision=lax.Precision.HIGHEST,
        preferred_element_type=jnp.float32,
    ).astype(jnp.bfloat16)
    turned = lax.all_to_all(spectra, "inp", split_axis=1, concat_axis=0, tiled=True)
    inputs = turned.shape[0]
    turned = turned.reshape(inputs, 2, ch_dev, spectra_dev)
    real_part = jnp.einsum("ipcs,jpcs->icj", turned, turned, preferred_element_type=jnp.float32)
    imag_part = jnp.einsum(
        "ics,jcs->icj", turned[:, 1], turned[:, 0], preferred_element_type=jnp.float32
    ) - jnp.einsum("ics,jcs->icj", turned[:, 0], turned[:, 1], preferred_element_type=jnp.float32)
    mine = lax.psum_scatter(
        jnp.stack([real_part, imag_part], axis=1), "tm", scatter_dimension=0, tiled=True
    )
    return mine * (1.0 / math.sqrt(spectra_dev * n_time))


def solution(mesh):
    return jax.shard_map(
        per_device,
        mesh=mesh,
        in_specs=(P("inp", "tm"), P()),
        out_specs=P("tm", None, "inp", None),
        check_vma=False,
    )
```

profile of v0, /device:TPU:0, one launch (start us, length us, event | category | flops | bytes accessed | tf_op | source)
XLA Modules:
  0.0 655.1 jit_solution(13122239102143808897)
XLA Ops:
  6.5 0.0 reduce-scatter.2.cloned.1.call-start
  6.5 0.0 copy-start.1
  6.5 9.3 %copy.28 = bf16[4,8,384,512]{3,2,1,0:T(8,128)(2,1)S(1)} copy(bf16[4,8,384,512]{3,1,2,0:T(8,128)(2,1)} %bitcast.50) | data formatting | bytes 25165824
  15.9 0.1 slice.42
  16.0 4.9 collective-permute-start
  20.9 4.3 fusion.79
  25.2 0.0 copy-done.1
  25.2 0.0 collective-permute-done
  25.2 51.8 %convert_bitcast_fusion = bf16[32,512,384]{2,1,0:T(8,128)(2,1)S(1)} fusion(bf16[32,384,512]{2,1,0:T(8,128)(2,1)S(1)} %bitcast.49, bf16[32,3,512]{2,1,0:T(4,128)(2,1)S(1)} %collective-permute-done, f32[512]{0:T(512)S(1)} %bitcast.53, f32[512]{0:T(512)S(1)} %bitcast.54, f32[512]{0:T(512)S(1)} %bitcast.52, f32[512]{0:T(512)S(1)} %bitcast.51, ...), kind=kOutput, calls=%fused_computation.24 | convolution fusion | flops 38786826240 | bytes 26320896 | tf_op jit(solution)/shard_map/isn,nj->ijs/dot_general | solution.py:43
  77.1 32.5 %copy.16 = bf16[32,512,384]{2,0,1:T(8,128)(2,1)S(1)} copy(bf16[32,512,384]{2,1,0:T(8,128)(2,1)S(1)} %convert_bitcast_fusion) | data formatting | bytes 25165824 | tf_op jit(solution)/shard_map/convert_element_type | solution.py:49
  109.6 278.4 %all_to_all.15 = bf16[32,512,384]{2,0,1:T(8,128)(2,1)S(1)} all-to-all(bf16[32,512,384]{2,0,1:T(8,128)(2,1)S(1)} %copy.16), channel_id=1, replica_groups=mesh['inp'=8,'tm'=4] {'inp'}, dimensions={1} | all-to-all | bytes 25165824 | tf_op jit(solution)/shard_map/all_to_all | solution.py:50
  388.0 14.8 %copy.18 = bf16[8,32,64,384]{3,2,1,0:T(8,128)(2,1)S(1)} copy(bf16[8,32,64,384]{3,1,2,0:T(8,128)(2,1)S(1)} %bitcast.47) | data formatting | bytes 25165824 | tf_op jit(solution)/shard_map/all_to_all | solution.py:50
  402.8 0.0 copy-start
  402.8 4.4 copy-done
  407.2 6.4 fusion.71
  413.6 20.0 %fusion.30 = f32[256,1,32,256]{0,3,2,1:T(8,128)} fusion(bf16[256,2,32,384]{3,2,1,0:T(8,128)(2,1)} %bitcast.46), kind=kOutput, calls=%fused_computation.34 | convolution fusion | flops 3221225472 | bytes 20971520 | tf_op jit(solution)/shard_map/ipcs,jpcs->icj/dot_general | solution.py:53
  433.6 11.5 %fusion.28 = f32[32,256,256]{2,1,0:T(8,128)} fusion(bf16[256,1,32,384]{3,2,1,0:T(8,128)(2,1)} %get-tuple-element.6, bf16[256,1,32,384]{3,2,1,0:T(8,128)(2,1)} %get-tuple-element.5), kind=kOutput, calls=%fused_computation.32 | convolution fusion | flops 1610612736 | bytes 20971520 | tf_op jit(solution)/shard_map/ics,jcs->icj/dot_general | solution.py:56
  445.2 14.1 %subtract_bitcast_fusion = f32[256,1,32,256]{0,3,2,1:T(8,128)} fusion(f32[32,256,256]{2,1,0:T(8,128)} %fusion.28, bf16[256,1,32,384]{3,2,1,0:T(8,128)(2,1)} %get-tuple-element.5, bf16[256,1,32,384]{3,2,1,0:T(8,128)(2,1)} %get-tuple-element.6), kind=kOutput, calls=%fused_computation.29 | convolution fusion | flops 1612709888 | bytes 29360128 | tf_op jit(solution)/shard_map/ics,jcs->icj/dot_general | solution.py:54
  459.2 11.5 %pad_maximum_fusion = f32[256,2,32,256]{0,3,2,1:T(8,128)} fusion(f32[256,1,32,256]{0,3,2,1:T(8,128)} %subtract_bitcast_fusion, f32[256,1,32,256]{0,3,2,1:T(8,128)} %fusion.30), kind=kLoop, calls=%fused_computation.14 | loop fusion | flops 4194304 | bytes 33554432 | tf_op jit(solution)/shard_map/stack | solution.py:58
  470.8 19.9 %copy.23 = f32[256,2,32,256]{3,2,1,0:T(8,128)} copy(f32[256,2,32,256]{0,3,2,1:T(8,128)} %pad_maximum_fusion) | data formatting | bytes 33554432 | tf_op jit(solution)/shard_map/stack | solution.py:58
  490.7 0.0 reduce-scatter.2.cloned.1.call-update
  490.7 152.1 %reduce-scatter.2.cloned.1.call-done = f32[64,2,32,256]{3,2,1,0:T(8,128)} async-done(((f32[256,2,32,256]{3,2,1,0:T(8,128)}), f32[64,2,32,256]{3,2,1,0:T(8,128)}) %reduce-scatter.2.cloned.1.call-update) | async-done | bytes 4194320 | tf_op jit(solution)/shard_map/reduce_scatter | solution.py:57
  642.9 5.1 broadcast_multiply_fusion
  (3 shorter events, 0.0 us)
Async XLA Ops:
  6.5 636.3 %reduce-scatter.2.cloned.1.call-start = ((), (), s32[]{:S(2)}) async-start(), calls=%async_computation.2 | async-start | bytes 20971520 | tf_op jit(solution)/shard_map/reduce_scatter | solution.py:57
  6.5 18.7 %copy-start.1 = (f32[4,512]{1,0:T(4,128)S(1)}, f32[4,512]{1,0:T(4,128)}, u32[]{:S(2)}) copy-start(f32[4,512]{1,0:T(4,128)} %param.3) | copy-start | bytes 24580
  16.0 9.3 %collective-permute-start = (bf16[32,3,512]{2,1,0:T(4,128)(2,1)S(1)}, bf16[32,3,512]{2,1,0:T(4,128)(2,1)S(1)}, u32[]{:S(2)}, u32[]{:S(2)}) collective-permute-start(bf16[32,3,512]{2,1,0:T(4,128)(2,1)S(1)} %slice.42), channel_id=1, source_target_pairs={{0,1},{1,2},{2,3},{4,5},{5,6},{6,7},{8,9},{9,10},{10,11},{12,13},{... | collective-permute-start | bytes 294920 | tf_op jit(solution)/shard_map/ppermute | solution.py:11
  402.8 4.5 copy-start
Sparse Core Ops, SparseCore 0:
  490.8 151.9 reduce-scatter.1
where the time goes:
time: 661 us; the launch traced here: 655 us
  blocking collectives  278 us (42%)
  waiting for transfers between devices  152 us (23%)
  matrix products  97.4 us (15%)
  local copies, waits for them, and re-layouts  87.5 us (13%)
  other arithmetic  21 us (3%)
  between operations  13.7 us (2%)
    all_to_all x1, blocking collectives, per_device(): lax.all_to_all(spectra, 'inp', split_axis=1, concat_axis=0, tiled=True)  278 us
    reduce_scatter x1, waiting for transfers between devices, per_device(): lax.psum_scatter(jnp.stack([real_part, imag_part], axis=1), 'tm', scatter...  152 us
    dot_general x1, matrix products, per_device(): jnp.einsum('isn,nj->ijs', filtered, table, precision=lax.Precision.HIGHES...  51.8 us
    convert_element_type x1, local copies, waits for them, and re-layouts, per_device(): spectra = jnp.einsum('isn,nj->ijs', filtered, table, precision=lax.Precis...  32.5 us
    dot_general x1, matrix products, per_device(): jnp.einsum('ipcs,jpcs->icj', turned, turned, preferred_element_type=jnp.f...  20 us
    another operation x1, local copies, waits for them, and re-layouts, per_device(): jnp.stack([real_part, imag_part], axis=1)  19.9 us
    all_to_all x1, local copies, waits for them, and re-layouts, per_device(): lax.all_to_all(spectra, 'inp', split_axis=1, concat_axis=0, tiled=True)  14.8 us
    dot_general x1, matrix products, per_device(): jnp.einsum('ics,jcs->icj', turned[:, 1], turned[:, 0], preferred_element_...  14.1 us
  transfers between devices with their start and end apart: 2, of which 1 were waited for; matrix products, arithmetic and copies ran while one was open for 1% of the time, Pallas kernels for 0%

commit v1 on v0

--- a/solution.py
+++ b/solution.py
@@ -47,7 +47,10 @@
         precision=lax.Precision.HIGHEST,
         preferred_element_type=jnp.float32,
     ).astype(jnp.bfloat16)
-    turned = lax.all_to_all(spectra, "inp", split_axis=1, concat_axis=0, tiled=True)
+    turned = jnp.concatenate(
+        lax.all_to_all(jnp.stack(jnp.split(spectra, lax.axis_size("inp"), axis=1)), "inp", 0, 0),
+        axis=0,
+    )
     inputs = turned.shape[0]
     turned = turned.reshape(inputs, 2, ch_dev, spectra_dev)
     real_part = jnp.einsum("ipcs,jpcs->icj", turned, turned, preferred_element_type=jnp.float32)

time: 661 us -> 616 us (0.932)
  local copies, waits for them, and re-layouts: 87.5 us -> 43.8 us
    convert_element_type x1 -> x0, local copies, waits for them, and re-layouts: 32.5 us -> none  [per_device(): spectra = jnp.einsum('isn,nj->ijs', filtered, table, precision=lax.Precis...]
    all_to_all x1 -> x0, local copies, waits for them, and re-layouts: 14.8 us -> none  [per_device(): lax.all_to_all(spectra, 'inp', split_axis=1, concat_axis=0, tiled=True)]
    unnamed x5 -> x12, local copies, waits for them, and re-layouts: 13.8 us -> 14.2 us
where the time goes in v1:
time: 616 us; the launch traced here: 610 us
  blocking collectives  279 us (45%)
  waiting for transfers between devices  152 us (25%)
  matrix products  96 us (16%)
  local copies, waits for them, and re-layouts  43.8 us (7%)
  other arithmetic  21 us (3%)
  between operations  13.8 us (2%)
    all_to_all x1, blocking collectives, per_device(): lax.all_to_all(jnp.stack(jnp.split(spectra, lax.axis_size('inp'), axis=1)...  279 us
    reduce_scatter x1, waiting for transfers between devices, per_device(): lax.psum_scatter(jnp.stack([real_part, imag_part], axis=1), 'tm', scatter...  152 us
    dot_general x1, matrix products, per_device(): jnp.einsum('isn,nj->ijs', filtered, table, precision=lax.Precision.HIGHES...  51.8 us
    dot_general x1, matrix products, per_device(): jnp.einsum('ipcs,jpcs->icj', turned, turned, preferred_element_type=jnp.f...  20 us
    another operation x1, local copies, waits for them, and re-layouts, per_device(): jnp.stack([real_part, imag_part], axis=1)  19.9 us
    unnamed x12, local copies, waits for them, and re-layouts  14.2 us
    dot_general x1, matrix products, per_device(): jnp.einsum('ics,jcs->icj', turned[:, 1], turned[:, 0], preferred_element_...  14.1 us
  transfers between devices with their start and end apart: 2, of which 1 were waited for; matrix products, arithmetic and copies ran while one was open for 1% of the time, Pallas kernels for 0%

profile of v1, /device:TPU:0, one launch (start us, length us, event | category | flops | bytes accessed | tf_op | source)
XLA Modules:
  0.0 610.1 jit_solution(9926496785697509962)
XLA Ops:
  6.5 0.0 reduce-scatter.2.cloned.1.call-start
  6.5 0.0 copy-start.1
  6.5 9.3 %copy.16 = bf16[4,8,384,512]{3,2,1,0:T(8,128)(2,1)S(1)} copy(bf16[4,8,384,512]{3,1,2,0:T(8,128)(2,1)} %bitcast.78) | data formatting | bytes 25165824
  15.9 0.1 slice.42
  16.0 4.9 collective-permute-start
  20.9 4.3 fusion.87
  25.2 0.0 copy-done.1
  25.2 0.0 collective-permute-done
  25.2 51.8 %convert_bitcast_fusion = bf16[32,512,384]{2,1,0:T(8,128)(2,1)S(1)} fusion(bf16[32,384,512]{2,1,0:T(8,128)(2,1)S(1)} %bitcast.77, bf16[32,3,512]{2,1,0:T(4,128)(2,1)S(1)} %collective-permute-done, f32[512]{0:T(512)S(1)} %bitcast.81, f32[512]{0:T(512)S(1)} %bitcast.82, f32[512]{0:T(512)S(1)} %bitcast.80, f32[512]{0:T(512)S(1)} %bitcast.79, ...), kind=kOutput, calls=%fused_computation.24 | convolution fusion | flops 38786826240 | bytes 26320896 | tf_op jit(solution)/shard_map/isn,nj->ijs/dot_general | solution.py:43
  77.1 0.2 fusion.40
  77.2 0.3 fusion.39
  77.6 0.3 fusion.38
  77.9 0.3 fusion.37
  78.3 0.3 fusion.36
  78.6 0.3 fusion.35
  79.0 0.3 fusion.34
  79.3 0.3 fusion.33
  79.7 278.5 %all_to_all.5 = bf16[8,32,64,384]{3,2,1,0:T(8,128)(2,1)} all-to-all(bf16[8,32,64,384]{3,2,1,0:T(8,128)(2,1)S(1)} %fusion.33), channel_id=1, replica_groups=mesh['inp'=8,'tm'=4] {'inp'}, dimensions={0} | all-to-all | bytes 25165824 | tf_op jit(solution)/shard_map/all_to_all | solution.py:51
  358.2 20.0 %fusion.30 = f32[256,1,32,256]{0,3,2,1:T(8,128)} fusion(bf16[256,2,32,384]{3,2,1,0:T(8,128)(2,1)} %bitcast.74), kind=kOutput, calls=%fused_computation.34 | convolution fusion | flops 3221225472 | bytes 20971520 | tf_op jit(solution)/shard_map/ipcs,jpcs->icj/dot_general | solution.py:56
  378.2 9.2 %fusion.79 = (bf16[256,1,32,384]{3,2,1,0:T(8,128)(2,1)S(1)}, bf16[256,1,32,384]{3,2,1,0:T(8,128)(2,1)}) fusion(bf16[256,2,32,384]{3,2,1,0:T(8,128)(2,1)} %bitcast.75), kind=kLoop, calls=%fused_computation.102 | loop fusion | bytes 25165824 | tf_op jit(solution)/shard_map/slice | solution.py:58
  387.4 0.0 copy-start
  387.4 2.6 copy-done
  390.1 10.2 %fusion.28 = f32[32,256,256]{2,1,0:T(8,128)} fusion(bf16[256,1,32,384]{3,2,1,0:T(8,128)(2,1)} %get-tuple-element.6, bf16[256,1,32,384]{3,2,1,0:T(8,128)(2,1)S(1)} %get-tuple-element.5), kind=kOutput, calls=%fused_computation.32 | convolution fusion | flops 1610612736 | bytes 20971520 | tf_op jit(solution)/shard_map/ics,jcs->icj/dot_general | solution.py:59
  400.2 14.1 %subtract_bitcast_fusion = f32[256,1,32,256]{0,3,2,1:T(8,128)} fusion(f32[32,256,256]{2,1,0:T(8,128)} %fusion.28, bf16[256,1,32,384]{3,2,1,0:T(8,128)(2,1)} %copy-done, bf16[256,1,32,384]{3,2,1,0:T(8,128)(2,1)} %get-tuple-element.6), kind=kOutput, calls=%fused_computation.29 | convolution fusion | flops 1612709888 | bytes 29360128 | tf_op jit(solution)/shard_map/ics,jcs->icj/dot_general | solution.py:57
  414.3 11.5 %pad_maximum_fusion = f32[256,2,32,256]{0,3,2,1:T(8,128)} fusion(f32[256,1,32,256]{0,3,2,1:T(8,128)} %subtract_bitcast_fusion, f32[256,1,32,256]{0,3,2,1:T(8,128)} %fusion.30), kind=kLoop, calls=%fused_computation.14 | loop fusion | flops 4194304 | bytes 33554432 | tf_op jit(solution)/shard_map/stack | solution.py:61
  425.8 19.9 %copy.12 = f32[256,2,32,256]{3,2,1,0:T(8,128)} copy(f32[256,2,32,256]{0,3,2,1:T(8,128)} %pad_maximum_fusion) | data formatting | bytes 33554432 | tf_op jit(solution)/shard_map/stack | solution.py:61
  445.8 0.0 reduce-scatter.2.cloned.1.call-update
  445.8 152.1 %reduce-scatter.2.cloned.1.call-done = f32[64,2,32,256]{3,2,1,0:T(8,128)} async-done(((f32[256,2,32,256]{3,2,1,0:T(8,128)}), f32[64,2,32,256]{3,2,1,0:T(8,128)}) %reduce-scatter.2.cloned.1.call-update) | async-done | bytes 4194320 | tf_op jit(solution)/shard_map/reduce_scatter | solution.py:60
  597.9 5.1 broadcast_multiply_fusion
  (3 shorter events, 0.0 us)
Async XLA Ops:
  6.5 591.4 %reduce-scatter.2.cloned.1.call-start = ((), (), s32[]{:S(2)}) async-start(), calls=%async_computation.2 | async-start | bytes 20971520 | tf_op jit(solution)/shard_map/reduce_scatter | solution.py:60
  6.5 18.7 %copy-start.1 = (f32[4,512]{1,0:T(4,128)S(1)}, f32[4,512]{1,0:T(4,128)}, u32[]{:S(2)}) copy-start(f32[4,512]{1,0:T(4,128)} %param.3) | copy-start | bytes 24580
  16.0 9.3 %collective-permute-start = (bf16[32,3,512]{2,1,0:T(4,128)(2,1)S(1)}, bf16[32,3,512]{2,1,0:T(4,128)(2,1)S(1)}, u32[]{:S(2)}, u32[]{:S(2)}) collective-permute-start(bf16[32,3,512]{2,1,0:T(4,128)(2,1)S(1)} %slice.42), channel_id=1, source_target_pairs={{0,1},{1,2},{2,3},{4,5},{5,6},{6,7},{8,9},{9,10},{10,11},{12,13},{... | collective-permute-start | bytes 294920 | tf_op jit(solution)/shard_map/ppermute | solution.py:11
  387.4 2.6 copy-start
Sparse Core Ops, SparseCore 0:
  445.9 151.9 reduce-scatter.1
